TPU v7x, 256 devices: a whole 4x4x8 slice. The times are simulated.
256 devices in a mesh: pole: 8 (over x, y_lo), sub: 32 (over y_hi, z, core).
Axes of the slice: x: 4, y: 4 (y_hi: 2, y_lo: 2; y = y_hi * 2 + y_lo), z: 8, core: 2. Of those that a mesh axis runs over, the one named last changes fastest.
Arguments:
- start_block: float32 [131072, 128], P('sub'), may hold values from -400 to 400
- inverses: float32 [8, 256, 512, 512], P('pole', 'sub'), may hold values from -1 to 3
- iface_rows: int32 [256, 2, 128], P('sub'), may hold values from 0 to 511, as said below
- neighbors: int32 [256, 2], P('sub'), may hold values from 0 to 255, as said below
- couplings: float32 [256, 2, 128], P('sub'), may hold values from 0.25 to 1
- pole_weights: float32 [8], P('pole'), may hold values from 0.25 to 1
Outputs:
- ortho_basis: float32 [131072, 128], P(('sub', 'pole'))
Inputs may be any that keep to these rules, and one draw needn't show every extreme that they name: `iface_rows`: in each subdomain the 256 listed rows are distinct. Subdomain j lies on index j // 8 of sub. neighbors[j, 0] lies on the previous index and neighbors[j, 1] on the next one, cyclically; over the subdomains of one index, the values in column 0 are the previous index's 8 subdomains, each once, and those in column 1 the next index's, each once.
All inputs are finite; a program needn't handle non-finite values.
Results may differ from a plain program's by a relative error of at most 0.0002.
Values sent between devices are 32-bit elements; how exact they have to be, the bound alone decides.
A program may use at most 64 MiB of HBM per device.

v0:
```python
import math
import jax
import jax.numpy as jnp
from jax import lax
from jax.sharding import PartitionSpec as P

precise = lax.Precision.HIGHEST


def extended_2(cells, sides, width):
    for axis, dim in sides:
        count = lax.axis_size(axis)
        head = lax.slice_in_dim(cells, 0, width, axis=dim)
        tail = lax.slice_in_dim(cells, cells.shape[dim] - width, cells.shape[dim], axis=dim)
        cells = jnp.concatenate(
            [
                lax.ppermute(tail, axis, [(i, (i + 1) % count) for i in range(count)]),
                cells,
                lax.ppermute(head, axis, [((i + 1) % count, i) for i in range(count)]),
            ],
            axis=dim,
        )
    return cells


def apply_blocks(blocks, fields):
    return jnp.einsum(
        "sij,sjv->siv", blocks, fields, precision=precise, preferred_element_type=jnp.float32
    )


def add_coupled(fields, iface_rows, neighbor_vals, couplings):

    def one_sub(field_one, rows_one, terms_one):
        field_one = field_one.at[rows_one[0]].add(terms_one[0])
        return field_one.at[rows_one[1]].add(terms_one[1])

    return jax.vmap(one_sub)(fields, iface_rows, couplings[..., None] * neighbor_vals)


def per_device(start_block, inverses, iface_rows, neighbors, couplings, pole_weights):
    blocks = inverses[0]
    sub_count = blocks.shape[0]
    block_len = blocks.shape[1]
    vec_count = start_block.shape[1]
    iface_len = iface_rows.shape[2]
    fields = start_block.reshape(sub_count, block_len, vec_count)
    first_pass = apply_blocks(blocks, fields)
    offsets = (jnp.arange(sub_count, dtype=jnp.int32) * block_len)[:, None, None]
    flat_index = (iface_rows + offsets).transpose(1, 0, 2).reshape(-1)
    outgoing = jnp.take(first_pass.reshape(sub_count * block_len, vec_count), flat_index, axis=0)
    half_rows = sub_count * iface_len
    extended = extended_2(outgoing, (("sub", 0),), half_rows)
    from_prev = extended[:half_rows].reshape(sub_count, iface_len, vec_count)
    from_next = extended[3 * half_rows :].reshape(sub_count, iface_len, vec_count)
    columns = jnp.arange(sub_count, dtype=jnp.int32)[None, :]
    choose_prev = (neighbors[:, 0:1] % sub_count == columns).astype(jnp.float32)
    choose_next = (neighbors[:, 1:2] % sub_count == columns).astype(jnp.float32)
    low_terms = jnp.einsum(
        "jk,kiv->jiv", choose_prev, from_prev, precision=precise, preferred_element_type=jnp.float32
    )
    high_terms = jnp.einsum(
        "jk,kiv->jiv", choose_next, from_next, precision=precise, preferred_element_type=jnp.float32
    )
    corrected = add_coupled(fields, iface_rows, jnp.stack([low_terms, high_terms], 1), couplings)
    weight = pole_weights[0]
    own_rows = sub_count * block_len // lax.axis_size("pole")
    pole_term = weight * apply_blocks(blocks, corrected).reshape(sub_count * block_len, vec_count)
    summed_poles = lax.psum(pole_term, "pole")
    filtered = lax.dynamic_slice_in_dim(
        summed_poles, lax.axis_index("pole") * own_rows, own_rows, 0
    )
    local_gram = jnp.dot(
        filtered.T, filtered, precision=precise, preferred_element_type=jnp.float32
    )
    gram_matrix = lax.psum(local_gram, ("pole", "sub"))
    lower_factor = jnp.linalg.cholesky(gram_matrix)
    total_rows = sub_count * block_len * lax.axis_size("sub")
    solved = lax.linalg.triangular_solve(
        lower_factor, filtered, left_side=False, lower=True, transpose_a=True
    )
    return math.sqrt(total_rows) * solved


def solution(mesh):
    placed = (
        P("sub", None),
        P("pole", "sub", None, None),
        P("sub", None, None),
        P("sub", None),
        P("sub", None, None),
        P("pole"),
    )
    return jax.shard_map(
        per_device, mesh=mesh, in_specs=placed, out_specs=P(("sub", "pole"), None), check_vma=False
    )
```

profile of v0, /device:TPU:1, one launch (start us, length us, event | category | flops | bytes accessed | tf_op | source)
XLA Modules:
  0.0 464.7 jit_solution(7205133361967697777)
XLA Ops:
  6.5 0.0 all-reduce.3.cloned.1.call-start
  6.5 1.6 copy.37
  8.1 0.0 copy-done
  8.1 0.1 compare_and_fusion
  8.3 10.6 %fusion.2 = f32[8,512,128]{2,1,0:T(8,128)} fusion(f32[8,512,128]{2,1,0:T(8,128)S(1)} %bitcast.62, f32[1,8,512,512]{3,2,1,0:T(8,128)} %param.7), kind=kOutput, calls=%fused_computation.5 | convolution fusion | flops 3221225472 | bytes 12582912 | tf_op jit(solution)/shard_map/sij,sjv->siv/dot_general | solution.py:27
  18.8 7.0 %gather_fusion = f32[2048,128]{1,0:T(8,128)S(1)} fusion(f32[4096,128]{1,0:T(8,128)} %bitcast.64, s32[2048]{0:T(1024)S(1)} %broadcast_clamp_fusion), kind=kCustom, calls=%fused_computation | custom fusion | bytes 2105344 | tf_op jit(solution)/shard_map/jit(_take)/gather | solution.py:51
  25.9 0.0 slice-start
  25.9 0.0 copy-start.2
  25.9 0.0 copy-start.3
  25.9 0.0 copy-start.1
  25.9 0.0 copy-start.4
  25.9 0.3 broadcast_select_fusion
  26.3 1.1 fusion.27
  27.3 3.2 collective-permute-start.1
  30.5 0.0 collective-permute-start
  30.6 0.0 slice-done
  30.6 0.0 copy-done.2
  30.6 0.0 copy-done.3
  30.6 0.1 multiply_reduce_fusion
  30.7 0.0 copy-done.1
  30.7 0.1 copy.12
  31.5 0.0 copy-done.4
  31.5 0.1 and_reduce_fusion
  31.6 5.8 %collective-permute-done.1 = f32[1024,128]{1,0:T(8,128)S(1)} collective-permute-done((f32[1024,128]{1,0:T(8,128)}, f32[1024,128]{1,0:T(8,128)S(1)}, u32[]{:S(2)}, u32[]{:S(2)}) %collective-permute-start.1) | collective-permute-done | bytes 524320 | tf_op jit(solution)/shard_map/ppermute | solution.py:19
  37.4 0.7 convolution_bitcast_fusion
  38.1 0.3 collective-permute-done
  38.4 0.7 convolution_bitcast_fusion.1
  39.0 0.3 maximum_multiply_fusion
  39.4 0.1 fusion.26
  39.5 0.1 copy.16
  39.6 0.1 copy.18
  39.7 6.8 %scatter_fusion = f32[4096,128]{1,0:T(8,128)S(1)} fusion(f32[4096,128]{1,0:T(8,128)S(1)} %copy.37, s32[1024]{0:T(1024)S(1)} %get-tuple-element.18, f32[1024,128]{1,0:T(8,128)S(1)} %bitcast.67), kind=kCustom, calls=%fused_computation.1 | custom fusion | flops 131072 | bytes 1576960
  46.5 7.0 %scatter_fusion.1 = f32[4096,128]{1,0:T(8,128)S(1)} fusion(f32[4096,128]{1,0:T(8,128)S(1)} %scatter_fusion, s32[1024]{0:T(1024)S(1)} %get-tuple-element.17, f32[1024,128]{1,0:T(8,128)S(1)} %bitcast.66), kind=kCustom, calls=%fused_computation.2 | custom fusion | flops 131072 | bytes 1576960
  53.5 12.6 %multiply_bitcast_fusion = f32[8,512,128]{1,2,0:T(8,128)} fusion(f32[8,512,128]{2,1,0:T(8,128)S(1)} %bitcast.63, f32[1,8,512,512]{3,2,1,0:T(8,128)} %param.7, f32[]{:T(128)} %bitcast.61), kind=kOutput, calls=%fused_computation.7 | convolution fusion | flops 3221749760 | bytes 12582916 | tf_op jit(solution)/shard_map/sij,sjv->siv/dot_general | solution.py:27
  66.1 2.9 copy.20
  69.0 0.0 all-reduce.3.cloned.1.call-update
  69.0 0.0 all-reduce.5.cloned.1.call-start
  69.1 113.2 %all-reduce.3.cloned.1.call-done = f32[4096,128]{1,0:T(8,128)} async-done(((f32[4096,128]{1,0:T(8,128)}), f32[4096,128]{1,0:T(8,128)}) %all-reduce.3.cloned.1.call-update) | async-done | bytes 2097168 | tf_op jit(solution)/shard_map/psum | solution.py:69
  182.3 2.2 fusion.9
  184.6 0.0 all-reduce.5.cloned.1.call-update
  184.6 246.6 %all-reduce.5.cloned.1.call-done = f32[128,128]{0,1:T(8,128)} async-done(((f32[128,128]{0,1:T(8,128)}), f32[128,128]{0,1:T(8,128)}) %all-reduce.5.cloned.1.call-update) | async-done | bytes 65552 | tf_op jit(solution)/shard_map/psum | solution.py:76
  431.2 0.9 copy.22
  432.1 0.9 fusion.13
  433.0 11.7 %cholesky.16 = f32[128,128]{1,0:T(8,128)S(1)} custom-call(f32[128,128]{1,0:T(8,128)S(1)} %fusion.13), custom_call_target="Cholesky" | custom-call | tf_op jit(solution)/shard_map/jit(cholesky)/cholesky | solution.py:77
  444.8 0.6 compare_reduce_fusion
  445.4 0.7 fusion.11
  446.1 9.8 %custom-call.6 = f32[1,128,128]{1,2,0:T(8,128)S(1)} custom-call(f32[1,128,128]{2,1,0:T(8,128)S(1)} %fusion.11), custom_call_target="InvertDiagBlocksLowerTriangular" | custom-call | tf_op jit(solution)/shard_map/triangular_solve | solution.py:79
  455.9 2.0 convolution_multiply_fusion
  (11 shorter events, 0.1 us)
Async XLA Ops:
  6.5 1.6 copy-start
  6.5 175.8 %all-reduce.3.cloned.1.call-start = ((), (), s32[]{:S(2)}) async-start(), calls=%async_computation | async-start | bytes 4194304 | tf_op jit(solution)/shard_map/psum | solution.py:69
  25.9 4.7 %slice-start = ((s32[8,2,128]{2,1,0:T(2,128)}), s32[8,1,128]{2,1,0:T(1,128)S(1)}, s32[]{:S(2)}) async-start(s32[8,2,128]{2,1,0:T(2,128)} %param.8), calls=%async_computation.2 | async-start | bytes 8192 | tf_op jit(solution)/shard_map/vmap()/slice | solution.py:35
  25.9 4.7 %copy-start.2 = (s32[8,2]{0,1:T(2,128)S(1)}, s32[8,2]{0,1:T(2,128)}, u32[]{:S(2)}) copy-start(s32[8,2]{0,1:T(2,128)} %param.9) | copy-start | bytes 196
  25.9 4.7 %copy-start.3 = (s32[2]{0:T(128)S(1)}, s32[2]{0:T(128)}, u32[]{:S(2)}) copy-start(s32[2]{0:T(128)} %constant.95) | copy-start | bytes 28
  25.9 4.8 %copy-start.1 = (f32[8,2,128]{2,1,0:T(2,128)S(1)}, f32[8,2,128]{2,1,0:T(2,128)}, u32[]{:S(2)}) copy-start(f32[8,2,128]{2,1,0:T(2,128)} %param.10) | copy-start | bytes 24580
  25.9 5.6 %copy-start.4 = (s32[2]{0:T(128)S(1)}, s32[2]{0:T(128)}, u32[]{:S(2)}) copy-start(s32[2]{0:T(128)} %constant.98) | copy-start | bytes 28
  27.3 10.1 %collective-permute-start.1 = (f32[1024,128]{1,0:T(8,128)}, f32[1024,128]{1,0:T(8,128)S(1)}, u32[]{:S(2)}, u32[]{:S(2)}) collective-permute-start(f32[1024,128]{1,0:T(8,128)} %get-tuple-element.14), channel_id=1, source_target_pairs={{1,0},{2,1},{3,2},{4,3},{5,4},{6,5},{7,6},{8,7},{9,8},{10,9},{11,1... | collective-permute-start | bytes 1572872 | tf_op jit(solution)/shard_map/ppermute | solution.py:19
  30.5 7.8 %collective-permute-start = (f32[1024,128]{1,0:T(8,128)}, f32[1024,128]{1,0:T(8,128)S(1)}, u32[]{:S(2)}, u32[]{:S(2)}) collective-permute-start(f32[1024,128]{1,0:T(8,128)} %get-tuple-element.13), channel_id=1, source_target_pairs={{0,1},{1,2},{2,3},{3,4},{4,5},{5,6},{6,7},{7,8},{8,9},{9,10},{10,1... | collective-permute-start | bytes 1572872 | tf_op jit(solution)/shard_map/ppermute | solution.py:17
  69.0 362.2 %all-reduce.5.cloned.1.call-start = ((), (), s32[]{:S(2)}) async-start(), calls=%async_computation.1 | async-start | bytes 131072 | tf_op jit(solution)/shard_map/psum | solution.py:76
Sparse Core Ops, SparseCore 0:
  69.2 113.1 all-reduce.2
  187.8 243.3 all-reduce.4
where the time goes:
time: 465 us
  waiting for transfers between devices  366 us (79%)
  other arithmetic  38.4 us (8%)
  matrix products  28.8 us (6%)
  between operations  14.3 us (3%)
  local copies, waits for them, and re-layouts  14 us (3%)
    psum x1, waiting for transfers between devices, per_device(): gram_matrix = lax.psum(local_gram, ('pole', 'sub'))  247 us
    psum x1, waiting for transfers between devices, per_device(): summed_poles = lax.psum(pole_term, 'pole')  113 us
    dot_general x2, matrix products, apply_blocks(): jnp.einsum('sij,sjv->siv', blocks, fields, precision=precise, preferred_e...  23.2 us
    unnamed x5, other arithmetic  13.9 us
    another operation x3, other arithmetic, per_device(): lower_factor = jnp.linalg.cholesky(gram_matrix)  12.4 us
    another operation x2, other arithmetic, per_device(): lax.linalg.triangular_solve(lower_factor, filtered, left_side=False, lowe...  10.5 us
  transfers between devices with their start and end apart: 4, of which 4 were waited for; matrix products, arithmetic and copies ran while one was open for 0% of the time, Pallas kernels for 0%

commit v1 on v0

--- a/solution.py
+++ b/solution.py
@@ -73,7 +73,7 @@
     local_gram = jnp.dot(
         filtered.T, filtered, precision=precise, preferred_element_type=jnp.float32
     )
-    gram_matrix = lax.psum(local_gram, ("pole", "sub"))
+    gram_matrix = jnp.sum(lax.all_gather(local_gram, ("pole", "sub")), axis=0)
     lower_factor = jnp.linalg.cholesky(gram_matrix)
     total_rows = sub_count * block_len * lax.axis_size("sub")
     solved = lax.linalg.triangular_solve(

time: 465 us -> 653 us (1.40)
  waiting for transfers between devices: 366 us -> 549 us
    all_gather x0 -> x1, waiting for transfers between devices: none -> 430 us  [per_device(): gram_matrix = jnp.sum(lax.all_gather(local_gram, ('pole', 'sub')), axis=0)]
    psum x1 -> x0, waiting for transfers between devices: 247 us -> none  [per_device(): gram_matrix = lax.psum(local_gram, ('pole', 'sub'))]
    reduce_sum x0 -> x1, other arithmetic: none -> 6.59 us  [per_device(): gram_matrix = jnp.sum(lax.all_gather(local_gram, ('pole', 'sub')), axis=0)]
where the time goes in v1:
time: 653 us
  waiting for transfers between devices  549 us (84%)
  other arithmetic  44.2 us (7%)
  matrix products  28.7 us (4%)
  between operations  14.3 us (2%)
  local copies, waits for them, and re-layouts  13.2 us (2%)
    all_gather x1, waiting for transfers between devices, per_device(): gram_matrix = jnp.sum(lax.all_gather(local_gram, ('pole', 'sub')), axis=0)  430 us
    psum x1, waiting for transfers between devices, per_device(): summed_poles = lax.psum(pole_term, 'pole')  111 us
    dot_general x2, matrix products, apply_blocks(): jnp.einsum('sij,sjv->siv', blocks, fields, precision=precise, preferred_e...  23.1 us
    unnamed x5, other arithmetic  13.9 us
  transfers between devices with their start and end apart: 4, of which 4 were waited for; matrix products, arithmetic and copies ran while one was open for 0% of the time, Pallas kernels for 0%

profile of v1, /device:TPU:1, one launch (start us, length us, event | category | flops | bytes accessed | tf_op | source)
XLA Modules:
  0.0 652.6 jit_solution(14692746117886193115)
XLA Ops:
  6.5 0.0 all-reduce.2.cloned.1.call-start
  6.5 1.6 copy.43
  8.1 0.0 copy-done
  8.1 0.1 compare_and_fusion
  8.3 10.6 %fusion.2 = f32[8,512,128]{2,1,0:T(8,128)} fusion(f32[8,512,128]{2,1,0:T(8,128)S(1)} %bitcast.63, f32[1,8,512,512]{3,2,1,0:T(8,128)} %param.7), kind=kOutput, calls=%fused_computation.5 | convolution fusion | flops 3221225472 | bytes 12582912 | tf_op jit(solution)/shard_map/sij,sjv->siv/dot_general | solution.py:27
  18.8 7.0 %gather_fusion = f32[2048,128]{1,0:T(8,128)S(1)} fusion(f32[4096,128]{1,0:T(8,128)} %bitcast.65, s32[2048]{0:T(1024)S(1)} %broadcast_clamp_fusion), kind=kCustom, calls=%fused_computation | custom fusion | bytes 2105344 | tf_op jit(solution)/shard_map/jit(_take)/gather | solution.py:51
  25.9 0.0 slice-start
  25.9 0.0 copy-start.2
  25.9 0.0 copy-start.3
  25.9 0.0 copy-start.1
  25.9 0.0 copy-start.4
  25.9 0.3 broadcast_select_fusion
  26.3 1.1 fusion.27
  27.3 3.0 collective-permute-start
  30.4 0.2 collective-permute-start.1
  30.5 0.0 slice-done
  30.6 0.0 copy-done.2
  30.6 0.0 copy-done.3
  30.6 0.1 multiply_reduce_fusion
  31.3 0.0 copy-done.1
  31.3 0.1 copy.21
  31.5 0.0 copy-done.4
  31.5 0.1 and_reduce_fusion
  31.6 5.2 collective-permute-done
  36.8 0.7 convolution_bitcast_fusion.1
  37.5 2.0 collective-permute-done.1
  39.5 0.7 convolution_bitcast_fusion
  40.1 0.3 maximum_multiply_fusion
  40.5 0.1 fusion.26
  40.6 0.1 copy.27
  40.7 0.1 copy.25
  40.8 6.8 %scatter_fusion = f32[4096,128]{1,0:T(8,128)S(1)} fusion(f32[4096,128]{1,0:T(8,128)S(1)} %copy.43, s32[1024]{0:T(1024)S(1)} %get-tuple-element.18, f32[1024,128]{1,0:T(8,128)S(1)} %bitcast.69), kind=kCustom, calls=%fused_computation.1 | custom fusion | flops 131072 | bytes 1576960
  47.6 7.0 %scatter_fusion.1 = f32[4096,128]{1,0:T(8,128)S(1)} fusion(f32[4096,128]{1,0:T(8,128)S(1)} %scatter_fusion, s32[1024]{0:T(1024)S(1)} %get-tuple-element.17, f32[1024,128]{1,0:T(8,128)S(1)} %bitcast.68), kind=kCustom, calls=%fused_computation.2 | custom fusion | flops 131072 | bytes 1576960
  54.6 12.6 %multiply_bitcast_fusion = f32[8,512,128]{1,2,0:T(8,128)} fusion(f32[8,512,128]{2,1,0:T(8,128)S(1)} %bitcast.64, f32[1,8,512,512]{3,2,1,0:T(8,128)} %param.7, f32[]{:T(128)} %bitcast.62), kind=kOutput, calls=%fused_computation.7 | convolution fusion | flops 3221749760 | bytes 12582916 | tf_op jit(solution)/shard_map/sij,sjv->siv/dot_general | solution.py:27
  67.2 2.9 copy.29
  70.1 0.0 all-reduce.2.cloned.1.call-update
  70.1 0.0 all-gather.3.cloned.1.call-start
  70.2 111.3 %all-reduce.2.cloned.1.call-done = f32[4096,128]{1,0:T(8,128)} async-done(((f32[4096,128]{1,0:T(8,128)}), f32[4096,128]{1,0:T(8,128)}) %all-reduce.2.cloned.1.call-update) | async-done | bytes 2097168 | tf_op jit(solution)/shard_map/psum | solution.py:69
  181.4 2.2 fusion.9
  183.7 0.0 all-gather.3.cloned.1.call-update
  183.7 430.5 %all-gather.3.cloned.1.call-done = f32[32768,128]{1,0:T(8,128)} async-done(((f32[128,128]{1,0:T(8,128)}), f32[32768,128]{1,0:T(8,128)}) %all-gather.3.cloned.1.call-update) | async-done | bytes 16777232 | tf_op jit(solution)/shard_map/all_gather | solution.py:76
  614.2 6.6 %reduce_sum.9 = f32[128,128]{1,0:T(8,128)S(1)} reduce(f32[256,128,128]{2,1,0:T(8,128)} %bitcast.66, f32[]{:T(128)} %constant.87.clone.1), dimensions={0}, to_apply=%region_3.4 | reduce | flops 4177920 | bytes 16842756 | tf_op jit(solution)/shard_map/reduce_sum | solution.py:76
  620.8 0.1 copy.30
  620.9 11.7 %cholesky.16 = f32[128,128]{1,0:T(8,128)S(1)} custom-call(f32[128,128]{1,0:T(8,128)S(1)} %fusion.13), custom_call_target="Cholesky" | custom-call | tf_op jit(solution)/shard_map/jit(cholesky)/cholesky | solution.py:77
  632.6 0.6 compare_reduce_fusion
  633.3 0.7 fusion.11
  633.9 9.8 %custom-call.6 = f32[1,128,128]{1,2,0:T(8,128)S(1)} custom-call(f32[1,128,128]{2,1,0:T(8,128)S(1)} %fusion.11), custom_call_target="InvertDiagBlocksLowerTriangular" | custom-call | tf_op jit(solution)/shard_map/triangular_solve | solution.py:79
  643.8 2.0 convolution_multiply_fusion
  (12 shorter events, 0.1 us)
Async XLA Ops:
  6.5 1.6 copy-start
  6.5 174.9 %all-reduce.2.cloned.1.call-start = ((), (), s32[]{:S(2)}) async-start(), calls=%async_computation | async-start | bytes 4194304 | tf_op jit(solution)/shard_map/psum | solution.py:69
  25.9 4.7 slice-start
  25.9 4.7 copy-start.2
  25.9 4.7 copy-start.3
  25.9 5.4 copy-start.1
  25.9 5.6 copy-start.4
  27.3 9.5 %collective-permute-start = (f32[1024,128]{1,0:T(8,128)}, f32[1024,128]{1,0:T(8,128)S(1)}, u32[]{:S(2)}, u32[]{:S(2)}) collective-permute-start(f32[1024,128]{1,0:T(8,128)} %get-tuple-element.13), channel_id=1, source_target_pairs={{0,1},{1,2},{2,3},{3,4},{4,5},{5,6},{6,7},{7,8},{8,9},{9,10},{10,1... | collective-permute-start | bytes 1572872 | tf_op jit(solution)/shard_map/ppermute | solution.py:17
  30.4 9.1 %collective-permute-start.1 = (f32[1024,128]{1,0:T(8,128)}, f32[1024,128]{1,0:T(8,128)S(1)}, u32[]{:S(2)}, u32[]{:S(2)}) collective-permute-start(f32[1024,128]{1,0:T(8,128)} %get-tuple-element.14), channel_id=1, source_target_pairs={{1,0},{2,1},{3,2},{4,3},{5,4},{6,5},{7,6},{8,7},{9,8},{10,9},{11,1... | collective-permute-start | bytes 1572872 | tf_op jit(solution)/shard_map/ppermute | solution.py:19
  70.1 544.1 %all-gather.3.cloned.1.call-start = ((), (), s32[]{:S(2)}) async-start(), calls=%async_computation.1 | async-start | bytes 16842752 | tf_op jit(solution)/shard_map/all_gather | solution.py:76
Sparse Core Ops, SparseCore 0:
  70.2 111.1 all-reduce.1
  183.8 430.3 all-gather.2
